TPU v7x, 256 devices: a whole 4x4x8 slice. The times are simulated.
256 devices in a mesh: chan: 8 (over y, core), row: 32 (over x, z).
Axes of the slice: x: 4, y: 4, z: 8, core: 2. Of those that a mesh axis runs over, the one named last changes fastest.
Arguments:
- voltages: bfloat16 [256, 2, 8, 1024], P('row', None, 'chan'), may hold values from -6 to 6
- kernels: float32 [256, 2, 4], P('row'), may hold values from 0.1 to 1.9
- footprint: int32 [256, 2], P('row'), may hold values from 0 to 252
- cal_weight: float32 [16, 8], P(None, 'chan'), may hold values from -6 to 6
Outputs:
- power_image: float32 [8, 256, 256], P('chan', None, 'row')
- calibrator_maps: float32 [16, 256, 256], P('chan', None, 'row')
All inputs are finite; a program needn't handle non-finite values.
Results may differ from a plain program's by a relative error of at most 0.004.
Values may be sent and summed in bfloat16 or wider, within the bound.
No kernel may reach another device: no remote copies, remote signals or barrier semaphores. Data moves between devices by JAX's collectives and lax.ppermute only.
A program may use at most 128 MiB of HBM per device.

v0:
```python
import math
import jax
import jax.numpy as jnp
from jax import lax
from jax.sharding import PartitionSpec as P

GRID = 256


def dft_tables(size, first, count):
    indices = jnp.arange(size, dtype=jnp.int32)
    columns = first + jnp.arange(count, dtype=jnp.int32)
    phases = indices[:, None] * columns[None, :] % size
    angles = phases.astype(jnp.float32) * (2.0 * math.pi / size)
    return (jnp.cos(angles), jnp.sin(angles))


def placed(weights, starts, count):
    positions = jnp.arange(count, dtype=jnp.int32)
    taps = jnp.arange(weights.shape[1], dtype=jnp.int32)
    target = starts[:, None] + taps[None, :]
    hit = positions[None, None, :] == target[:, :, None]
    return jnp.sum(jnp.where(hit, weights[:, :, None], jnp.zeros((), weights.dtype)), axis=1)


def blocked_time_sum(values):
    samples = values.shape[-1]
    width = math.gcd(samples, 128)
    shaped = values.reshape(values.shape[:-1] + (samples // width, width))
    return jnp.sum(jnp.sum(shaped, axis=-1), axis=-1)


def image_columns(block):
    highest = lax.Precision.HIGHEST
    cos_table, sin_table = dft_tables(block.shape[1], 0, block.shape[1])
    half_real = block[0]
    half_imag = block[1]
    sky_real = jnp.einsum("umx,ul->lmx", half_real, cos_table, precision=highest) + jnp.einsum(
        "umx,ul->lmx", half_imag, sin_table, precision=highest
    )
    sky_imag = jnp.einsum("umx,ul->lmx", half_imag, cos_table, precision=highest) - jnp.einsum(
        "umx,ul->lmx", half_real, sin_table, precision=highest
    )
    return jnp.stack([sky_real, sky_imag])


def on_device(voltages, kernels, footprint, cal_weight):
    highest = lax.Precision.HIGHEST
    local_stations, _, local_channels, samples = voltages.shape
    row_count = lax.axis_size("row")
    grid_size = GRID
    row_share = grid_size // row_count
    first_row = lax.axis_index("row") * row_share
    columns_total = local_channels * samples
    kernel_taps = kernels.shape[2]
    station_count = local_stations * row_count
    power_scale = 1.0 / (2.0 * samples * station_count * kernel_taps * kernel_taps)
    volt_flat = voltages.reshape(local_stations, 2, columns_total)
    volt_all, kern_all, foot_all = (
        lax.all_gather(volt_flat, "row", axis=0, tiled=True),
        lax.all_gather(kernels.astype(jnp.bfloat16), "row", axis=0, tiled=True).astype(
            kernels.dtype
        ),
        lax.all_gather(footprint, "row", axis=0, tiled=True),
    )
    row_weight = placed(kern_all[:, 0, :], foot_all[:, 0], grid_size)
    col_weight = placed(kern_all[:, 1, :], foot_all[:, 1], grid_size)
    cos_local, sin_local = dft_tables(grid_size, first_row, row_share)
    resp_real = jnp.dot(col_weight, cos_local, precision=highest)
    resp_imag = -jnp.dot(col_weight, sin_local, precision=highest)
    volt_values = volt_all.astype(jnp.float32)
    volt_real = volt_values[:, 0, :]
    volt_imag = volt_values[:, 1, :]
    term_real = (
        resp_real[:, :, None] * volt_real[:, None, :]
        - resp_imag[:, :, None] * volt_imag[:, None, :]
    )
    term_imag = (
        resp_real[:, :, None] * volt_imag[:, None, :]
        + resp_imag[:, :, None] * volt_real[:, None, :]
    )
    terms = jnp.stack([term_real, term_imag], axis=1)
    half_image = jnp.einsum("su,skmx->kumx", row_weight, terms, precision=highest)
    sky = image_columns(half_image)
    squared = sky[0] * sky[0] + sky[1] * sky[1]
    squared = squared.reshape(grid_size, row_share, local_channels, samples)
    power_image = jnp.transpose(blocked_time_sum(squared) * power_scale, (2, 0, 1))
    calibrator_maps = lax.psum_scatter(
        jnp.einsum("qc,clm->qlm", cal_weight, power_image, precision=highest),
        "chan",
        scatter_dimension=0,
        tiled=True,
    )
    return (power_image, calibrator_maps)


def solution(mesh):
    placed = (P("row", None, "chan", None), P("row", None, None), P("row", None), P(None, "chan"))
    return jax.shard_map(
        on_device,
        mesh=mesh,
        in_specs=placed,
        out_specs=(P("chan", None, "row"), P("chan", None, "row")),
        check_vma=False,
    )
```

profile of v0, /device:TPU:2, one launch (start us, length us, event | category | flops | bytes accessed | tf_op | source)
XLA Modules:
  0.0 228.4 jit_solution(15883283409992685155)
XLA Ops:
  7.2 0.7 all-gather.4.cloned.1.call-update
  7.9 0.7 convert_element_type.22
  8.6 0.1 copy.42
  8.7 45.6 %all-gather.1 = s32[32,8,2]{1,2,0:T(2,128)S(1)} all-gather(s32[1,8,2]{1,2,0:T(2,128)} %bitcast.52), channel_id=1, replica_groups=mesh['chan'=8,'row'=32] {'row'}, dimensions={0}, use_global_device_ids=true | all-gather | bytes 2112 | tf_op jit(solution)/shard_map/all_gather | solution.py:64
  54.3 0.1 reshape.103
  54.4 41.1 %all_gather.10 = bf16[256,2,4]{2,1,0:T(2,128)(2,1)S(1)} all-gather(bf16[8,2,4]{2,1,0:T(2,128)(2,1)S(1)} %copy.42), channel_id=1, replica_groups=mesh['chan'=8,'row'=32] {'row'}, dimensions={0}, use_global_device_ids=true | all-gather | bytes 4224 | tf_op jit(solution)/shard_map/all_gather | solution.py:61
  95.5 0.2 fusion.66
  95.9 0.3 select_reduce_fusion.1
  96.3 0.3 select_reduce_fusion
  96.6 0.8 convolution_negate_fusion
  97.4 0.9 fusion.26
  98.3 2.0 bitcast_convert_fusion
  100.3 1.6 fusion.65
  101.9 1.1 copy.56
  103.0 1.0 copy.57
  104.0 4.2 %multiply_subtract_fusion = (f32[256,1,8,1024]{0,3,2,1:T(8,128)S(1)}, f32[256,1,8,1024]{0,3,2,1:T(8,128)}) fusion(f32[256,1024]{0,1:T(8,128)S(1)} %bitcast.47, f32[256,8]{0,1:T(8,128)S(1)} %convolution_negate_fusion, f32[256,1024]{0,1:T(8,128)S(1)} %bitcast.46, f32[256,8]{0,1:T(8,128)S(1)} %fusion.26), kind=kLoop, calls=%fused_computation.8 | loop fusion | flops 12582912 | bytes 18890752 | tf_op jit(solution)/shard_map/sub | solution.py:75
  108.2 17.8 %fusion.8 = f32[2,256,8,1024]{1,3,2,0:T(8,128)} fusion(f32[256,1,8,1024]{0,3,2,1:T(8,128)} %get-tuple-element.3, f32[256,1,8,1024]{0,3,2,1:T(8,128)S(1)} %get-tuple-element.2, f32[256,256]{1,0:T(8,128)S(1)} %select_reduce_fusion), kind=kOutput, calls=%fused_computation.13 | convolution fusion | flops 12889096192 | bytes 33816576 | tf_op jit(solution)/shard_map/su,skmx->kumx/dot_general | solution.py:83
  126.0 13.4 %fusion.6 = f32[256,8,1024]{2,0,1:T(8,128)S(1)} fusion(f32[2,256,8,1024]{1,3,2,0:T(8,128)} %fusion.8), kind=kOutput, calls=%fused_computation.11 | convolution fusion | flops 6443368448 | bytes 16777216 | tf_op jit(solution)/shard_map/umx,ul->lmx/dot_general | solution.py:41
  139.5 11.7 %fusion.4 = f32[256,8,1024]{2,0,1:T(8,128)} fusion(f32[2,256,8,1024]{1,3,2,0:T(8,128)S(1)} %copy-done), kind=kOutput, calls=%fused_computation.9 | convolution fusion | flops 6443368448 | bytes 16777216 | tf_op jit(solution)/shard_map/umx,ul->lmx/dot_general | solution.py:41
  151.2 11.4 %fusion.5 = f32[256,8,1024]{2,0,1:T(8,128)} fusion(f32[2,256,8,1024]{1,3,2,0:T(8,128)S(1)} %copy-done), kind=kOutput, calls=%fused_computation.10 | convolution fusion | flops 6443368448 | bytes 16777216 | tf_op jit(solution)/shard_map/umx,ul->lmx/dot_general | solution.py:38
  162.6 25.1 %add_reduce_fusion = f32[256,8]{0,1:T(8,128)S(1)} fusion(f32[256,8,1024]{2,0,1:T(8,128)S(1)} %fusion.6, f32[256,8,1024]{2,0,1:T(8,128)} %fusion.4, f32[256,8,1024]{2,0,1:T(8,128)} %fusion.5, f32[2,256,8,1024]{1,3,2,0:T(8,128)} %fusion.8), kind=kOutput, calls=%fused_computation.6 | convolution fusion | flops 6455949312 | bytes 33562624 | tf_op jit(solution)/shard_map/umx,ul->lmx/dot_general | solution.py:38
  187.7 0.6 broadcast_multiply_fusion
  188.3 0.7 multiply_bitcast_fusion
  189.1 32.4 %reduce-scatter.2.cloned.1.call-done = f32[2,256,8]{1,2,0:T(8,128)} async-done(((f32[16,256,8]{1,2,0:T(8,128)}), f32[2,256,8]{1,2,0:T(8,128)}) %reduce-scatter.2.cloned.1.call-update) | async-done | bytes 16400 | tf_op jit(solution)/shard_map/reduce_scatter | solution.py:88
  (15 shorter events, 0.3 us)
Async XLA Ops:
  7.2 91.1 %all-gather.4.cloned.1.call-start = ((), (), s32[]{:S(2)}) async-start(), calls=%async_computation.2 | async-start | bytes 1081344 | tf_op jit(solution)/shard_map/all_gather | solution.py:60
  7.9 213.6 %reduce-scatter.2.cloned.1.call-start = ((), (), s32[]{:S(2)}) async-start(), calls=%async_computation.1 | async-start | bytes 147456 | tf_op jit(solution)/shard_map/reduce_scatter | solution.py:88
  126.0 13.5 %copy-start = (f32[2,256,8,1024]{1,3,2,0:T(8,128)S(1)}, f32[2,256,8,1024]{1,3,2,0:T(8,128)}, u32[]{:S(2)}) copy-start(f32[2,256,8,1024]{1,3,2,0:T(8,128)} %fusion.8) | copy-start | bytes 50331652
  162.6 25.7 %copy-start.1 = (f32[16,1]{0,1:T(1,128)S(1)}, f32[16,1]{0,1:T(1,128)}, u32[]{:S(2)}) copy-start(f32[16,1]{0,1:T(1,128)} %param.7) | copy-start | bytes 196
Sparse Core Ops, SparseCore 0:
  10.6 78.1 all-gather.3
  189.2 32.2 reduce-scatter.1
where the time goes:
time: 229 us; the launch traced here: 228 us
  blocking collectives  86.7 us (38%)
  matrix products  81.1 us (35%)
  waiting for transfers between devices  33.1 us (14%)
  between operations  14.1 us (6%)
  other arithmetic  8.93 us (4%)
  local copies, waits for them, and re-layouts  4.26 us (2%)
    all_gather x1, blocking collectives, on_device(): lax.all_gather(footprint, 'row', axis=0, tiled=True)  45.6 us
    all_gather x1, blocking collectives, on_device(): lax.all_gather(kernels.astype(jnp.bfloat16), 'row', axis=0, tiled=True)  41.1 us
    reduce_scatter x1, waiting for transfers between devices, on_device(): lax.psum_scatter(jnp.einsum('qc,clm->qlm', cal_weight, power_image, preci...  32.4 us
    dot_general x1, matrix products, image_columns(): jnp.einsum('umx,ul->lmx', half_imag, sin_table, precision=highest)  25.1 us
    dot_general x1, matrix products, on_device(): jnp.einsum('su,skmx->kumx', row_weight, terms, precision=highest)  17.8 us
    dot_general x1, matrix products, image_columns(): jnp.einsum('umx,ul->lmx', half_imag, cos_table, precision=highest)  13.4 us
    dot_general x1, matrix products, image_columns(): jnp.einsum('umx,ul->lmx', half_real, sin_table, precision=highest)  11.7 us
    dot_general x1, matrix products, image_columns(): jnp.einsum('umx,ul->lmx', half_real, cos_table, precision=highest)  11.4 us
  transfers between devices with their start and end apart: 2, of which 1 were waited for; matrix products, arithmetic and copies ran while one was open for 2% of the time, Pallas kernels for 0%

commit v1 on v0

--- a/solution.py
+++ b/solution.py
@@ -61,7 +61,9 @@
         lax.all_gather(kernels.astype(jnp.bfloat16), "row", axis=0, tiled=True).astype(
             kernels.dtype
         ),
-        lax.all_gather(footprint, "row", axis=0, tiled=True),
+        jnp.concatenate(
+            lax.all_to_all(jnp.stack([footprint] * lax.axis_size("row")), "row", 0, 0), axis=0
+        ),
     )
     row_weight = placed(kern_all[:, 0, :], foot_all[:, 0], grid_size)
     col_weight = placed(kern_all[:, 1, :], foot_all[:, 1], grid_size)

time: 229 us -> 219 us (0.956)
  blocking collectives: 86.7 us -> 42.8 us
  waiting for transfers between devices: 33.1 us -> 54.3 us
  starting transfers between devices: 0.08 us -> 11.7 us
    all_gather x1 -> x0, blocking collectives: 45.6 us -> none  [on_device(): lax.all_gather(footprint, 'row', axis=0, tiled=True)]
    all_gather x1, waiting for transfers between devices: 0.01 us -> 21.5 us  [on_device(): lax.all_gather(volt_flat, 'row', axis=0, tiled=True)]
    all_to_all x0 -> x1, starting transfers between devices: none -> 11.6 us  [on_device(): lax.all_to_all(jnp.stack([footprint] * lax.axis_size('row')), 'row', 0, 0)]
  transfers between devices with their start and end apart: 2 -> 3, of which waited for: 1 -> 2; matrix products, arithmetic and copies ran while one was open for 2% -> 2% of each run, Pallas kernels for 0% -> 0%
where the time goes in v1:
time: 219 us; the launch traced here: 218 us
  matrix products  81.2 us (37%)
  waiting for transfers between devices  54.3 us (25%)
  blocking collectives  42.8 us (20%)
  between operations  14.1 us (6%)
  starting transfers between devices  11.7 us (5%)
  other arithmetic  8.88 us (4%)
  local copies, waits for them, and re-layouts  5.57 us (3%)
    all_gather x1, blocking collectives, on_device(): lax.all_gather(kernels.astype(jnp.bfloat16), 'row', axis=0, tiled=True)  42.8 us
    reduce_scatter x1, waiting for transfers between devices, on_device(): lax.psum_scatter(jnp.einsum('qc,clm->qlm', cal_weight, power_image, preci...  32.1 us
    dot_general x1, matrix products, image_columns(): jnp.einsum('umx,ul->lmx', half_imag, sin_table, precision=highest)  25.1 us
    all_gather x1, waiting for transfers between devices, on_device(): lax.all_gather(volt_flat, 'row', axis=0, tiled=True)  21.5 us
    dot_general x1, matrix products, on_device(): jnp.einsum('su,skmx->kumx', row_weight, terms, precision=highest)  17.8 us
    dot_general x1, matrix products, image_columns(): jnp.einsum('umx,ul->lmx', half_imag, cos_table, precision=highest)  13.4 us
    dot_general x1, matrix products, image_columns(): jnp.einsum('umx,ul->lmx', half_real, sin_table, precision=highest)  11.8 us
    all_to_all x1, starting transfers between devices, on_device(): lax.all_to_all(jnp.stack([footprint] * lax.axis_size('row')), 'row', 0, 0)  11.6 us
  transfers between devices with their start and end apart: 3, of which 2 were waited for; matrix products, arithmetic and copies ran while one was open for 2% of the time, Pallas kernels for 0%

profile of v1, /device:TPU:2, one launch (start us, length us, event | category | flops | bytes accessed | tf_op | source)
XLA Modules:
  0.0 218.5 jit_solution(8874965925855977712)
XLA Ops:
  7.2 0.7 all-gather.3.cloned.1.call-update
  7.9 1.3 stack.4
  9.2 11.6 %all-to-all-start = ((s32[32,8,2]{1,2,0:T(2,128)}), s32[32,8,2]{1,2,0:T(2,128)S(1)}, u32[]{:S(2)}, u32[]{:S(2)}) async-start(s32[32,8,2]{1,2,0:T(2,128)} %stack.4), calls=%async_computation | async-start | bytes 65536 | tf_op jit(solution)/shard_map/all_to_all | solution.py:65
  20.9 0.7 convert_element_type.22
  21.7 42.8 %all_gather.6 = bf16[256,2,4]{2,1,0:T(2,128)(2,1)S(1)} all-gather(bf16[8,2,4]{2,1,0:T(2,128)(2,1)S(1)} %copy.50), channel_id=1, replica_groups=mesh['chan'=8,'row'=32] {'row'}, dimensions={0}, use_global_device_ids=true | all-gather | bytes 4224 | tf_op jit(solution)/shard_map/all_gather | solution.py:61
  64.4 0.2 fusion.66
  64.9 0.3 select_reduce_fusion.1
  65.3 0.3 select_reduce_fusion
  65.6 0.8 convolution_negate_fusion
  66.4 0.9 fusion.26
  67.3 21.5 %all-gather.3.cloned.1.call-done = bf16[256,2,1,1024]{3,1,2,0:T(2,128)(2,1)} async-done(((bf16[8,2,1,1024]{3,1,2,0:T(2,128)(2,1)}), bf16[256,2,1,1024]{3,1,2,0:T(2,128)(2,1)}) %all-gather.3.cloned.1.call-update) | async-done | bytes 1048592 | tf_op jit(solution)/shard_map/all_gather | solution.py:60
  88.7 1.9 bitcast_convert_fusion
  90.7 1.6 fusion.65
  92.3 1.1 copy.64
  93.5 1.0 copy.65
  94.4 4.2 %multiply_subtract_fusion = (f32[256,1,8,1024]{0,3,2,1:T(8,128)S(1)}, f32[256,1,8,1024]{0,3,2,1:T(8,128)}) fusion(f32[256,1024]{0,1:T(8,128)S(1)} %bitcast.46, f32[256,8]{0,1:T(8,128)S(1)} %convolution_negate_fusion, f32[256,1024]{0,1:T(8,128)S(1)} %bitcast.45, f32[256,8]{0,1:T(8,128)S(1)} %fusion.26), kind=kLoop, calls=%fused_computation.8 | loop fusion | flops 12582912 | bytes 18890752 | tf_op jit(solution)/shard_map/sub | solution.py:77
  98.6 17.8 %fusion.8 = f32[2,256,8,1024]{1,3,2,0:T(8,128)} fusion(f32[256,1,8,1024]{0,3,2,1:T(8,128)} %get-tuple-element.3, f32[256,1,8,1024]{0,3,2,1:T(8,128)S(1)} %get-tuple-element.2, f32[256,256]{1,0:T(8,128)S(1)} %select_reduce_fusion), kind=kOutput, calls=%fused_computation.13 | convolution fusion | flops 12889096192 | bytes 33816576 | tf_op jit(solution)/shard_map/su,skmx->kumx/dot_general | solution.py:85
  116.5 13.4 %fusion.6 = f32[256,8,1024]{2,0,1:T(8,128)S(1)} fusion(f32[2,256,8,1024]{1,3,2,0:T(8,128)} %fusion.8), kind=kOutput, calls=%fused_computation.11 | convolution fusion | flops 6443368448 | bytes 16777216 | tf_op jit(solution)/shard_map/umx,ul->lmx/dot_general | solution.py:41
  129.9 11.8 %fusion.4 = f32[256,8,1024]{2,0,1:T(8,128)} fusion(f32[2,256,8,1024]{1,3,2,0:T(8,128)S(1)} %copy-done), kind=kOutput, calls=%fused_computation.9 | convolution fusion | flops 6443368448 | bytes 16777216 | tf_op jit(solution)/shard_map/umx,ul->lmx/dot_general | solution.py:41
  141.7 11.4 %fusion.5 = f32[256,8,1024]{2,0,1:T(8,128)} fusion(f32[2,256,8,1024]{1,3,2,0:T(8,128)S(1)} %copy-done), kind=kOutput, calls=%fused_computation.10 | convolution fusion | flops 6443368448 | bytes 16777216 | tf_op jit(solution)/shard_map/umx,ul->lmx/dot_general | solution.py:38
  153.1 25.1 %add_reduce_fusion = f32[256,8]{0,1:T(8,128)S(1)} fusion(f32[256,8,1024]{2,0,1:T(8,128)S(1)} %fusion.6, f32[256,8,1024]{2,0,1:T(8,128)} %fusion.4, f32[256,8,1024]{2,0,1:T(8,128)} %fusion.5, f32[2,256,8,1024]{1,3,2,0:T(8,128)} %fusion.8), kind=kOutput, calls=%fused_computation.6 | convolution fusion | flops 6455949312 | bytes 33562624 | tf_op jit(solution)/shard_map/umx,ul->lmx/dot_general | solution.py:38
  178.2 0.6 broadcast_multiply_fusion
  178.8 0.7 multiply_bitcast_fusion
  179.6 32.1 %reduce-scatter.2.cloned.1.call-done = f32[2,256,8]{1,2,0:T(8,128)} async-done(((f32[16,256,8]{1,2,0:T(8,128)}), f32[2,256,8]{1,2,0:T(8,128)}) %reduce-scatter.2.cloned.1.call-update) | async-done | bytes 16400 | tf_op jit(solution)/shard_map/reduce_scatter | solution.py:90
  (17 shorter events, 0.5 us)
Async XLA Ops:
  7.2 81.6 %all-gather.3.cloned.1.call-start = ((), (), s32[]{:S(2)}) async-start(), calls=%async_computation.3 | async-start | bytes 1081344 | tf_op jit(solution)/shard_map/all_gather | solution.py:60
  9.2 55.6 %all-to-all-start = ((s32[32,8,2]{1,2,0:T(2,128)}), s32[32,8,2]{1,2,0:T(2,128)S(1)}, u32[]{:S(2)}, u32[]{:S(2)}) async-start(s32[32,8,2]{1,2,0:T(2,128)} %stack.4), calls=%async_computation | async-start | bytes 65536 | tf_op jit(solution)/shard_map/all_to_all | solution.py:65
  20.8 190.8 %reduce-scatter.2.cloned.1.call-start = ((), (), s32[]{:S(2)}) async-start(), calls=%async_computation.2 | async-start | bytes 147456 | tf_op jit(solution)/shard_map/reduce_scatter | solution.py:90
  116.5 13.5 %copy-start = (f32[2,256,8,1024]{1,3,2,0:T(8,128)S(1)}, f32[2,256,8,1024]{1,3,2,0:T(8,128)}, u32[]{:S(2)}) copy-start(f32[2,256,8,1024]{1,3,2,0:T(8,128)} %fusion.8) | copy-start | bytes 50331652
  153.1 25.7 %copy-start.1 = (f32[16,1]{0,1:T(1,128)S(1)}, f32[16,1]{0,1:T(1,128)}, u32[]{:S(2)}) copy-start(f32[16,1]{0,1:T(1,128)} %param.7) | copy-start | bytes 196
Sparse Core Ops, SparseCore 0:
  10.6 78.1 all-gather.2
  179.7 31.9 reduce-scatter.1
